TPU v7x, 32 devices: a whole 2x2x4 slice. The times are simulated.
32 devices in a mesh: dp: 8 (over y, x, core), tp: 4 (over z).
Axes of the slice: x: 2, y: 2, z: 4, core: 2. Of those that a mesh axis runs over, the one named last changes fastest.
Arguments:
- tokens: bfloat16 [20480, 768], P(('dp', 'tp')), may hold values from -6 to 6
- w_query: bfloat16 [768, 768], P('dp', 'tp'), may hold values from -0.3125 to 0.3125
- w_key: bfloat16 [768, 768], P('dp', 'tp'), may hold values from -0.3125 to 0.3125
- w_value: bfloat16 [768, 768], P('dp', 'tp'), may hold values from -0.21875 to 0.21875
- b_query: bfloat16 [768], P('dp'), may hold values from -3 to 3
- b_value: bfloat16 [768], P('dp'), may hold values from -3 to 3
- w_out: bfloat16 [768, 768], P('dp', 'tp'), may hold values from -0.875 to 0.875
- b_out: bfloat16 [768], P('dp'), may hold values from -3 to 3
- gain_attn: bfloat16 [768], P('dp'), may hold values from 0.25 to 1.75
- shift_attn: bfloat16 [768], P('dp'), may hold values from -3 to 3
- w_up: bfloat16 [768, 3072], P('dp', 'tp'), may hold values from -0.21875 to 0.21875
- b_up: bfloat16 [3072], P('dp'), may hold values from -3 to 3
- w_down: bfloat16 [768, 3072], P('dp', 'tp'), may hold values from -0.15625 to 0.15625
- b_down: bfloat16 [768], P('dp'), may hold values from -3 to 3
- gain_ffn: bfloat16 [768], P('dp'), may hold values from 0.25 to 1.75
- shift_ffn: bfloat16 [768], P('dp'), may hold values from -3 to 3
- lengths: int32 [16], replicated, may hold values from 1024 to 1536, as said below
- deal_order: int32 [16], replicated, may hold values from 0 to 15, as said below
- cotangent: bfloat16 [20480, 768], P(('dp', 'tp')), may hold values from -6 to 6
Outputs:
- encoder_output: bfloat16 [20480, 768], P(('dp', 'tp'))
- grad_tokens: float32 [20480, 768], P(('dp', 'tp'))
- grad_w_query: float32 [768, 768], P('dp', 'tp')
- grad_w_key: float32 [768, 768], P('dp', 'tp')
- grad_w_value: float32 [768, 768], P('dp', 'tp')
- grad_b_query: float32 [768], P('dp')
- grad_b_value: float32 [768], P('dp')
- grad_w_out: float32 [768, 768], P('dp', 'tp')
- grad_b_out: float32 [768], P('dp')
- grad_gain_attn: float32 [768], P('dp')
- grad_shift_attn: float32 [768], P('dp')
- grad_w_up: float32 [768, 3072], P('dp', 'tp')
- grad_b_up: float32 [3072], P('dp')
- grad_w_down: float32 [768, 3072], P('dp', 'tp')
- grad_b_down: float32 [768], P('dp')
- grad_gain_ffn: float32 [768], P('dp')
- grad_shift_ffn: float32 [768], P('dp')
Inputs may be any that keep to these rules, and one draw needn't show every extreme that they name: Group g holds sequence deal_order[2 g] in slot 0 and deal_order[2 g + 1] in slot 1; the two lengths of a group add up to 2560, and each is at least 1024. `deal_order`: each of 0 to 15 appears once.
All inputs are finite; a program needn't handle non-finite values.
Results may differ from a plain program's by a relative error of at most 0.015.
The roundings to bfloat16 on the way count: a program that leaves them out, or rounds other values in their place, can miss the bound.
Values may be sent and summed in bfloat16 or wider, within the bound.
A program may use at most 128 MiB of HBM per device.

v0:
```python
import jax
import jax.numpy as jnp
from jax import lax
from jax.sharding import PartitionSpec as P

HD = 64
EPS = 1e-05
SQRT_HALF = 0.7071067811865476
INV_ROOT_TAU = 0.3989422804014327


def normalize_layer(resid):
    center = resid - jnp.mean(resid, axis=-1, keepdims=True)
    inverse_deviation = lax.rsqrt(jnp.mean(center * center, axis=-1, keepdims=True) + EPS)
    return (center * inverse_deviation, inverse_deviation)


def normalize_backward(output_gradient, centered_scaled, inverse_deviation, norm_gain):
    scaled_rows = output_gradient * norm_gain
    return inverse_deviation * (
        scaled_rows
        - jnp.mean(scaled_rows, axis=-1, keepdims=True)
        - centered_scaled * jnp.mean(scaled_rows * centered_scaled, axis=-1, keepdims=True)
    )


def gelu_slope(pre_act):
    return (
        0.5 * (1.0 + lax.erf(pre_act * SQRT_HALF))
        + pre_act * jnp.exp(-0.5 * pre_act * pre_act) * INV_ROOT_TAU
    )


def contract_last(left, right):
    return lax.dot_general(
        left, right, (((1,), (1,)), ((), ())), preferred_element_type=jnp.float32
    )


def contract_first(left, right):
    return lax.dot_general(
        left, right, (((0,), (0,)), ((), ())), preferred_element_type=jnp.float32
    )


def body(
    tokens,
    w_query,
    w_key,
    w_value,
    b_query,
    b_value,
    w_out,
    b_out,
    gain_attn,
    shift_attn,
    w_up,
    b_up,
    w_down,
    b_down,
    gain_ffn,
    shift_ffn,
    lengths,
    deal_order,
    cotangent,
):
    own_rows = tokens.shape[0]
    tp_index = lax.axis_index("tp")
    group_rows = own_rows * lax.axis_size("tp")
    params = (
        w_query,
        w_key,
        w_value,
        w_out,
        w_up,
        w_down,
        b_query,
        b_value,
        b_out,
        gain_attn,
        shift_attn,
        b_up,
        b_down,
        gain_ffn,
        shift_ffn,
    )
    gathered = (
        lax.all_gather(params[0], "dp", axis=0, tiled=True),
        lax.all_gather(params[1], "dp", axis=0, tiled=True),
        lax.all_gather(params[2], "dp", axis=0, tiled=True),
        lax.all_gather(params[3], "dp", axis=0, tiled=True),
        lax.all_gather(params[4], "dp", axis=0, tiled=True),
        lax.all_gather(params[5], "dp", axis=0, tiled=True),
        lax.all_gather(params[6], "dp", axis=0, tiled=True),
        lax.all_gather(params[7], "dp", axis=0, tiled=True),
        lax.all_gather(params[8], "dp", axis=0, tiled=True),
        lax.all_gather(params[9], "dp", axis=0, tiled=True),
        lax.all_gather(params[10], "dp", axis=0, tiled=True),
        lax.all_gather(params[11], "dp", axis=0, tiled=True),
        lax.all_gather(params[12], "dp", axis=0, tiled=True),
        lax.all_gather(params[13], "dp", axis=0, tiled=True),
        lax.all_gather(params[14], "dp", axis=0, tiled=True),
    )
    (
        query_weight,
        key_weight,
        value_weight,
        out_weight,
        up_weight,
        down_weight,
        query_bias,
        value_bias,
        out_bias,
        first_norm_gain,
        first_norm_shift,
        up_bias,
        down_projection_bias,
        second_norm_gain,
        second_norm_shift,
    ) = gathered
    width = query_weight.shape[1]
    hidden_width = up_weight.shape[1]
    heads = width // HD
    block = min(512, group_rows)
    blocks = group_rows // block
    scale = HD ** (-0.5)
    pair = lax.dynamic_slice_in_dim(deal_order, 2 * lax.axis_index("dp"), 2)
    first_len = jnp.sum(
        jnp.where(jnp.arange(lengths.shape[0], dtype=jnp.int32) == pair[0], lengths, 0)
    )
    segment = (jnp.arange(group_rows, dtype=jnp.int32) >= first_len).astype(jnp.int32)
    own_query_bias = lax.dynamic_slice_in_dim(query_bias, tp_index * width, width).astype(
        jnp.float32
    )
    own_value_bias = lax.dynamic_slice_in_dim(value_bias, tp_index * width, width).astype(
        jnp.float32
    )
    own_up_bias = lax.dynamic_slice_in_dim(up_bias, tp_index * hidden_width, hidden_width).astype(
        jnp.float32
    )
    input_full = lax.all_gather(tokens, "tp", axis=0, tiled=True)
    query_rows = (
        jnp.dot(input_full, query_weight, preferred_element_type=jnp.float32) + own_query_bias
    ).astype(jnp.bfloat16)
    key_rows = jnp.dot(input_full, key_weight, preferred_element_type=jnp.float32).astype(
        jnp.bfloat16
    )
    value_rows = (
        jnp.dot(input_full, value_weight, preferred_element_type=jnp.float32) + own_value_bias
    ).astype(jnp.bfloat16)
    key_heads = key_rows.reshape(group_rows, heads, HD)
    value_heads = value_rows.reshape(group_rows, heads, HD)
    query_blocks = query_rows.reshape(blocks, block, heads, HD)
    seg_blocks = segment.reshape(blocks, block)

    def masked_scores(query_block, seg_block):
        scores = (
            jnp.einsum("qhd,khd->hqk", query_block, key_heads, preferred_element_type=jnp.float32)
            * scale
        )
        allowed = seg_block[:, None] == segment[None, :]
        return jnp.where(allowed[None], scores, -1e30)

    def attend(inputs):
        query_block, seg_block = inputs
        scores = masked_scores(query_block, seg_block)
        highest = jnp.max(scores, axis=-1, keepdims=True)
        raised = jnp.exp(scores - highest)
        total = jnp.sum(raised, axis=-1, keepdims=True)
        shares = (raised / total).astype(jnp.bfloat16)
        mixed = jnp.einsum("hqk,khd->qhd", shares, value_heads, preferred_element_type=jnp.float32)
        return (
            mixed.astype(jnp.bfloat16).reshape(block, width),
            (highest + jnp.log(total))[:, :, 0],
        )

    mixed_blocks, log_totals = lax.map(attend, (query_blocks, seg_blocks))
    mixed_rows = mixed_blocks.reshape(group_rows, width)
    attn_term = lax.psum_scatter(
        contract_last(mixed_rows, out_weight), "tp", scatter_dimension=0, tiled=True
    )
    first_residual = tokens.astype(jnp.float32) + attn_term + out_bias.astype(jnp.float32)
    first_centered_scaled, first_inverse_deviation = normalize_layer(first_residual)
    normalized_rows = first_centered_scaled * first_norm_gain.astype(
        jnp.float32
    ) + first_norm_shift.astype(jnp.float32)
    normed_full = lax.all_gather(normalized_rows.astype(jnp.bfloat16), "tp", axis=0, tiled=True)
    pre_act = jnp.dot(normed_full, up_weight, preferred_element_type=jnp.float32) + own_up_bias
    hidden = jax.nn.gelu(pre_act, approximate=False).astype(jnp.bfloat16)
    feedforward_term = lax.psum_scatter(
        contract_last(hidden, down_weight), "tp", scatter_dimension=0, tiled=True
    )
    second_centered_scaled, second_inverse_deviation = normalize_layer(
        normalized_rows + feedforward_term + down_projection_bias.astype(jnp.float32)
    )
    encoder_output = (
        second_centered_scaled * second_norm_gain.astype(jnp.float32)
        + second_norm_shift.astype(jnp.float32)
    ).astype(jnp.bfloat16)
    gathered = (
        lax.all_gather(params[0], "dp", axis=0, tiled=True),
        lax.all_gather(params[1], "dp", axis=0, tiled=True),
        lax.all_gather(params[2], "dp", axis=0, tiled=True),
        lax.all_gather(params[3], "dp", axis=0, tiled=True),
        lax.all_gather(params[4], "dp", axis=0, tiled=True),
        lax.all_gather(params[5], "dp", axis=0, tiled=True),
        lax.all_gather(params[6], "dp", axis=0, tiled=True),
        lax.all_gather(params[7], "dp", axis=0, tiled=True),
        lax.all_gather(params[8], "dp", axis=0, tiled=True),
        lax.all_gather(params[9], "dp", axis=0, tiled=True),
        lax.all_gather(params[10], "dp", axis=0, tiled=True),
        lax.all_gather(params[11], "dp", axis=0, tiled=True),
        lax.all_gather(params[12], "dp", axis=0, tiled=True),
        lax.all_gather(params[13], "dp", axis=0, tiled=True),
        lax.all_gather(params[14], "dp", axis=0, tiled=True),
    )
    (
        query_weight,
        key_weight,
        value_weight,
        out_weight,
        up_weight,
        down_weight,
        query_bias,
        value_bias,
        out_bias,
        first_norm_gain,
        first_norm_shift,
        up_bias,
        down_projection_bias,
        second_norm_gain,
        second_norm_shift,
    ) = gathered
    output_gradient = cotangent.astype(jnp.float32)
    second_gain_gradient = jnp.sum(output_gradient * second_centered_scaled, axis=0)
    grad_shift_two = jnp.sum(output_gradient, axis=0)
    second_residual_gradient = normalize_backward(
        output_gradient,
        second_centered_scaled,
        second_inverse_deviation,
        second_norm_gain.astype(jnp.float32),
    )
    grad_ffn_full = lax.all_gather(
        second_residual_gradient.astype(jnp.bfloat16), "tp", axis=0, tiled=True
    )
    grad_down_bias = jnp.sum(grad_ffn_full, axis=0, dtype=jnp.float32)
    grad_down_weight = contract_first(grad_ffn_full, hidden)
    grad_hidden = jnp.dot(grad_ffn_full, down_weight, preferred_element_type=jnp.float32)
    grad_pre = (grad_hidden * gelu_slope(pre_act)).astype(jnp.bfloat16)
    grad_up_bias = jnp.sum(grad_pre, axis=0, dtype=jnp.float32)
    grad_up_weight = contract_first(normed_full, grad_pre)
    normalized_gradient = second_residual_gradient + lax.psum_scatter(
        contract_last(grad_pre, up_weight), "tp", scatter_dimension=0, tiled=True
    )
    first_gain_gradient = jnp.sum(normalized_gradient * first_centered_scaled, axis=0)
    grad_shift_one = jnp.sum(normalized_gradient, axis=0)
    first_residual_gradient = normalize_backward(
        normalized_gradient,
        first_centered_scaled,
        first_inverse_deviation,
        first_norm_gain.astype(jnp.float32),
    )
    grad_attn_full = lax.all_gather(
        first_residual_gradient.astype(jnp.bfloat16), "tp", axis=0, tiled=True
    )
    grad_out_bias = jnp.sum(grad_attn_full, axis=0, dtype=jnp.float32)
    grad_out_weight = contract_first(grad_attn_full, mixed_rows)
    grad_mixed = jnp.dot(grad_attn_full, out_weight, preferred_element_type=jnp.float32).astype(
        jnp.bfloat16
    )

    def attend_back(carry, inputs):
        key_grad, value_grad = carry
        query_block, seg_block, total_block, grad_block = inputs
        scores = masked_scores(query_block, seg_block)
        shares = jnp.exp(scores - total_block[:, :, None])
        grad_shares = jnp.einsum(
            "qhd,khd->hqk", grad_block, value_heads, preferred_element_type=jnp.float32
        )
        centre = jnp.sum(shares * grad_shares, axis=-1, keepdims=True)
        grad_scores = (shares * (grad_shares - centre)).astype(jnp.bfloat16)
        query_grad = (
            jnp.einsum("hqk,khd->qhd", grad_scores, key_heads, preferred_element_type=jnp.float32)
            * scale
        )
        key_grad = (
            key_grad
            + jnp.einsum(
                "hqk,qhd->khd", grad_scores, query_block, preferred_element_type=jnp.float32
            )
            * scale
        )
        value_grad = value_grad + jnp.einsum(
            "hqk,qhd->khd",
            shares.astype(jnp.bfloat16),
            grad_block,
            preferred_element_type=jnp.float32,
        )
        return ((key_grad, value_grad), query_grad.astype(jnp.bfloat16).reshape(block, width))

    zero_heads = jnp.zeros((group_rows, heads, HD), jnp.float32)
    (key_grad, value_grad), query_grads = lax.scan(
        attend_back,
        (zero_heads, zero_heads),
        (query_blocks, seg_blocks, log_totals, grad_mixed.reshape(blocks, block, heads, HD)),
    )
    grad_query = query_grads.reshape(group_rows, width)
    grad_key = key_grad.astype(jnp.bfloat16).reshape(group_rows, width)
    grad_value = value_grad.astype(jnp.bfloat16).reshape(group_rows, width)
    grad_query_weight = contract_first(input_full, grad_query)
    grad_key_weight = contract_first(input_full, grad_key)
    grad_value_weight = contract_first(input_full, grad_value)
    total = contract_last(grad_query, query_weight)
    total = total + contract_last(grad_key, key_weight)
    back_term = lax.psum_scatter(
        (total + contract_last(grad_value, value_weight)).astype(jnp.bfloat16),
        "tp",
        scatter_dimension=0,
        tiled=True,
    ).astype(jnp.float32)
    grad_tokens = first_residual_gradient + back_term
    empty_model = jnp.zeros((query_bias.shape[0],), jnp.float32)
    query_bias_grad = lax.dynamic_update_slice_in_dim(
        empty_model, jnp.sum(grad_query, axis=0, dtype=jnp.float32), tp_index * width, 0
    )
    value_bias_grad = lax.dynamic_update_slice_in_dim(
        empty_model, jnp.sum(grad_value, axis=0, dtype=jnp.float32), tp_index * width, 0
    )
    up_bias_grad = lax.dynamic_update_slice_in_dim(
        jnp.zeros((up_bias.shape[0],), jnp.float32), grad_up_bias, tp_index * hidden_width, 0
    )
    (
        query_bias_grad,
        value_bias_grad,
        up_bias_grad,
        first_gain_gradient,
        grad_shift_one,
        second_gain_gradient,
        grad_shift_two,
    ) = lax.psum(
        (
            query_bias_grad,
            value_bias_grad,
            up_bias_grad,
            first_gain_gradient,
            grad_shift_one,
            second_gain_gradient,
            grad_shift_two,
        ),
        "tp",
    )
    owned = (
        lax.psum_scatter(grad_query_weight, "dp", scatter_dimension=0, tiled=True),
        lax.psum_scatter(grad_key_weight, "dp", scatter_dimension=0, tiled=True),
        lax.psum_scatter(grad_value_weight, "dp", scatter_dimension=0, tiled=True),
        lax.psum_scatter(grad_out_weight, "dp", scatter_dimension=0, tiled=True),
        lax.psum_scatter(grad_up_weight, "dp", scatter_dimension=0, tiled=True),
        lax.psum_scatter(grad_down_weight, "dp", scatter_dimension=0, tiled=True),
        lax.psum_scatter(query_bias_grad, "dp", scatter_dimension=0, tiled=True),
        lax.psum_scatter(value_bias_grad, "dp", scatter_dimension=0, tiled=True),
        lax.psum_scatter(grad_out_bias, "dp", scatter_dimension=0, tiled=True),
        lax.psum_scatter(first_gain_gradient, "dp", scatter_dimension=0, tiled=True),
        lax.psum_scatter(grad_shift_one, "dp", scatter_dimension=0, tiled=True),
        lax.psum_scatter(up_bias_grad, "dp", scatter_dimension=0, tiled=True),
        lax.psum_scatter(grad_down_bias, "dp", scatter_dimension=0, tiled=True),
        lax.psum_scatter(second_gain_gradient, "dp", scatter_dimension=0, tiled=True),
        lax.psum_scatter(grad_shift_two, "dp", scatter_dimension=0, tiled=True),
    )
    return (
        encoder_output,
        grad_tokens,
        owned[0],
        owned[1],
        owned[2],
        owned[6],
        owned[7],
        owned[3],
        owned[8],
        owned[9],
        owned[10],
        owned[4],
        owned[11],
        owned[5],
        owned[12],
        owned[13],
        owned[14],
    )


def solution(mesh):
    in_specs = (
        P(("dp", "tp"), None),
        P("dp", "tp"),
        P("dp", "tp"),
        P("dp", "tp"),
        P("dp"),
        P("dp"),
        P("dp", "tp"),
        P("dp"),
        P("dp"),
        P("dp"),
        P("dp", "tp"),
        P("dp"),
        P("dp", "tp"),
        P("dp"),
        P("dp"),
        P("dp"),
        P(),
        P(),
        P(("dp", "tp"), None),
    )
    out_specs = (
        P(("dp", "tp"), None),
        P(("dp", "tp"), None),
        P("dp", "tp"),
        P("dp", "tp"),
        P("dp", "tp"),
        P("dp"),
        P("dp"),
        P("dp", "tp"),
        P("dp"),
        P("dp"),
        P("dp"),
        P("dp", "tp"),
        P("dp"),
        P("dp", "tp"),
        P("dp"),
        P("dp"),
        P("dp"),
    )
    return jax.shard_map(body, mesh=mesh, in_specs=in_specs, out_specs=out_specs, check_vma=False)
```

profile of v0, /device:TPU:0, one launch (start us, length us, event | category | flops | bytes accessed | tf_op | source)
XLA Modules:
  0.0 1452.7 jit_solution(7568280337318745953)
XLA Ops:
  18.3 27.4 %all-reduce.19 = (bf16[768]{0:T(1024)(128)(2,1)S(1)}, bf16[768]{0:T(1024)(128)(2,1)S(1)}, bf16[768]{0:T(1024)(128)(2,1)}, bf16[768]{0:T(1024)(128)(2,1)}, bf16[7...) all-reduce(bf16[768]{0:T(1024)(128)(2,1)S(1)} %dynamic-update-slice, ...), channel_id=1, replica_groups=mesh['dp'=8,'tp'=4] {'dp'}, use_global_device_ids=true, to_apply=%add | all-reduce | flops 6144 | bytes 24576
  72.6 10.4 all_gather.71
  103.4 72.3 %while.28 = (s32[]{:T(128)}, bf16[5,512,192]{1,2,0:T(8,128)(2,1)}, f32[5,3,512]{2,1,0:T(4,128)S(1)}, s32[5,512]{1,0:T(8,128)S(1)}, bf16[5,512,3,64]{1,3,2,0:T(8,...) while((s32[]{:T(128)}, bf16[5,512,192]{1,2,0:T(8,128)(2,1)}, ...), condition=%wide.region_4.5_spmd.clone, body=%wide.region_1.4_spmd.clone.sunk | while | flops 1055231488 | bytes 55263352 | solution.py:177
  185.3 133.9 %reduce-scatter.17.cloned.1.call-done = f32[640,768]{1,0:T(8,128)} async-done(((f32[2560,768]{1,0:T(8,128)}), f32[640,768]{1,0:T(8,128)}) %reduce-scatter.17.cloned.1.call-update) | async-done | bytes 1966096 | tf_op jit(solution)/shard_map/reduce_scatter | solution.py:179
  332.7 67.2 %all-gather.10.cloned.1.call-done = bf16[2560,768]{1,0:T(8,128)(2,1)} async-done(((bf16[640,768]{1,0:T(8,128)(2,1)}), bf16[2560,768]{1,0:T(8,128)(2,1)}) %all-gather.10.cloned.1.call-update) | async-done | bytes 3932176 | tf_op jit(solution)/shard_map/all_gather | solution.py:187
  399.9 22.3 %fusion.42 = (bf16[2560,768]{1,0:T(8,128)(2,1)}, f32[2560,768]{1,0:T(8,128)}) fusion(f32[768]{0:T(1024)S(1)} %dynamic-slice_convert_fusion, bf16[2560,768]{1,0:T(8,128)(2,1)} %all-gather.10.cloned.1.call-done, bf16[768,768]{1,0:T(8,128)(2,1)} %all-gather.12.cloned.1.call-done), kind=kOutput, calls=%fused_computation.56 | convolution fusion | flops 3149660160 | bytes 16911360 | tf_op jit(solution)/shard_map/dot_general | solution.py:188
  433.6 135.6 %reduce-scatter.19.cloned.1.call-done = f32[640,768]{1,0:T(8,128)} async-done(((f32[2560,768]{1,0:T(8,128)}), f32[640,768]{1,0:T(8,128)}) %reduce-scatter.19.cloned.1.call-update) | async-done | bytes 1966096 | tf_op jit(solution)/shard_map/reduce_scatter | solution.py:190
  575.1 77.0 %all-gather.16.cloned.1.call-done = bf16[2560,768]{1,0:T(8,128)(2,1)} async-done(((bf16[640,768]{1,0:T(8,128)(2,1)}), bf16[2560,768]{1,0:T(8,128)(2,1)}) %all-gather.16.cloned.1.call-update) | async-done | bytes 3932176 | tf_op jit(solution)/shard_map/all_gather | solution.py:243
  652.1 9.7 convert_reduce_fusion.1
  669.8 134.2 %reduce-scatter.21.cloned.1.call-done = f32[640,768]{1,0:T(8,128)} async-done(((f32[2560,768]{1,0:T(8,128)}), f32[640,768]{1,0:T(8,128)}) %reduce-scatter.21.cloned.1.call-update) | async-done | bytes 1966096 | tf_op jit(solution)/shard_map/reduce_scatter | solution.py:252
  812.2 76.9 %all-gather.18.cloned.1.call-done = bf16[2560,768]{1,0:T(8,128)(2,1)} async-done(((bf16[640,768]{1,0:T(8,128)(2,1)}), bf16[2560,768]{1,0:T(8,128)(2,1)}) %all-gather.18.cloned.1.call-update) | async-done | bytes 3932176 | tf_op jit(solution)/shard_map/all_gather | solution.py:263
  898.4 215.4 %while.29 = (s32[]{:T(128)}, f32[2560,3,64]{0,2,1:T(8,128)}, f32[2560,3,64]{0,2,1:T(8,128)}, bf16[5,512,192]{1,2,0:T(8,128)(2,1)}, bf16[5,512,3,64]{1,3,2,0:T(8,...) while((s32[]{:T(128)}, f32[2560,3,64]{0,2,1:T(8,128)}, ...), condition=%wide.region_18.19_spmd.clone, body=%wide.region_16.18_spmd.clone.sunk | while | flops 2555940352 | bytes 180019440 | solution.py:302
  917.7 9.5 multiply_convert_fusion.2
  960.2 9.5 multiply_convert_fusion.2
  1003.4 9.5 multiply_convert_fusion.2
  1046.7 9.5 multiply_convert_fusion.2
  1089.9 9.5 multiply_convert_fusion.2
  1168.5 25.8 %all-reduce.17 = (f32[768]{0:T(1024)S(1)}, f32[768]{0:T(1024)S(1)}, f32[768]{0:T(1024)S(1)}, f32[768]{0:T(1024)S(1)}, f32[768]{0:T(1024)S(1)}, /*index=5*/f32[30...) all-reduce(f32[768]{0:T(1024)S(1)} %dynamic_update_slice.20, ...), channel_id=9, replica_groups=mesh['dp'=8,'tp'=4] {'dp'}, use_global_device_ids=true, to_apply=%region_25.26.clone | all-reduce | flops 9216 | bytes 73728
  1207.7 36.4 %reduce-scatter.27.cloned.1.call-done = f32[96,768]{1,0:T(8,128)} async-done(((f32[768,768]{1,0:T(8,128)}), f32[96,768]{1,0:T(8,128)}) %reduce-scatter.27.cloned.1.call-update) | async-done | bytes 294928 | tf_op jit(solution)/shard_map/reduce_scatter | solution.py:357
  1244.1 46.3 %reduce-scatter.29.cloned.1.call-done = f32[96,768]{1,0:T(8,128)} async-done(((f32[768,768]{1,0:T(8,128)}), f32[96,768]{1,0:T(8,128)}) %reduce-scatter.29.cloned.1.call-update) | async-done | bytes 294928 | tf_op jit(solution)/shard_map/reduce_scatter | solution.py:358
  1290.4 38.7 %reduce-scatter.25.cloned.1.call-done = f32[96,192]{1,0:T(8,128)} async-done(((f32[768,192]{1,0:T(8,128)}), f32[96,192]{1,0:T(8,128)}) %reduce-scatter.25.cloned.1.call-update) | async-done | bytes 73744 | tf_op jit(solution)/shard_map/reduce_scatter | solution.py:356
  1329.1 38.7 %reduce-scatter.31.cloned.1.call-done = f32[96,192]{1,0:T(8,128)} async-done(((f32[768,192]{1,0:T(8,128)}), f32[96,192]{1,0:T(8,128)}) %reduce-scatter.31.cloned.1.call-update) | async-done | bytes 73744
  1367.8 38.6 %reduce-scatter.33.cloned.1.call-done = f32[96,192]{1,0:T(8,128)} async-done(((f32[768,192]{1,0:T(8,128)}), f32[96,192]{1,0:T(8,128)}) %reduce-scatter.33.cloned.1.call-update) | async-done | bytes 73744
  1406.4 38.7 %reduce-scatter.35.cloned.1.call-done = f32[96,192]{1,0:T(8,128)} async-done(((f32[768,192]{1,0:T(8,128)}), f32[96,192]{1,0:T(8,128)}) %reduce-scatter.35.cloned.1.call-update) | async-done | bytes 73744
  (323 shorter events, 428.5 us)
Async XLA Ops:
  8.0 81.6 %all-gather.8.cloned.1.call-start = ((), (), s32[]{:S(2)}) async-start(), calls=%async_computation.10 | async-start | bytes 4915200 | tf_op jit(solution)/shard_map/all_gather | solution.py:141
  8.8 310.4 %reduce-scatter.17.cloned.1.call-start = ((), (), s32[]{:S(2)}) async-start(), calls=%async_computation.11 | async-start | bytes 9830400 | tf_op jit(solution)/shard_map/reduce_scatter | solution.py:179
  54.5 39.6 %copy-start.19 = (bf16[768,192]{1,0:T(8,128)(2,1)}, bf16[768,192]{1,0:T(8,128)(2,1)S(1)}, u32[]{:S(2)}) copy-start(bf16[768,192]{1,0:T(8,128)(2,1)S(1)} %all_gather.66) | copy-start | bytes 884740
  63.7 33.5 %copy-start.14 = (bf16[768,192]{1,0:T(8,128)(2,1)}, bf16[768,192]{1,0:T(8,128)(2,1)S(1)}, u32[]{:S(2)}) copy-start(bf16[768,192]{1,0:T(8,128)(2,1)S(1)} %all_gather.68) | copy-start | bytes 884740
  72.6 28.4 %copy-start.17 = (bf16[768,192]{1,0:T(8,128)(2,1)}, bf16[768,192]{1,0:T(8,128)(2,1)S(1)}, u32[]{:S(2)}) copy-start(bf16[768,192]{1,0:T(8,128)(2,1)S(1)} %all_gather.69) | copy-start | bytes 884740
  184.2 148.5 %all-gather.12.cloned.1.call-start = ((), (), s32[]{:S(2)}) async-start(), calls=%async_computation.13 | async-start | bytes 1327104 | tf_op jit(solution)/shard_map/all_gather | solution.py:92
  184.8 215.2 %all-gather.10.cloned.1.call-start = ((), (), s32[]{:S(2)}) async-start(), calls=%async_computation.12 | async-start | bytes 4915200 | tf_op jit(solution)/shard_map/all_gather | solution.py:187
  323.0 101.0 %all-gather.14.cloned.1.call-start = ((), (), s32[]{:S(2)}) async-start(), calls=%async_computation.14 | async-start | bytes 1327104 | tf_op jit(solution)/shard_map/all_gather | solution.py:93
  323.6 245.7 %reduce-scatter.19.cloned.1.call-start = ((), (), s32[]{:S(2)}) async-start(), calls=%async_computation.15 | async-start | bytes 9830400 | tf_op jit(solution)/shard_map/reduce_scatter | solution.py:190
  432.9 219.2 %all-gather.16.cloned.1.call-start = ((), (), s32[]{:S(2)}) async-start(), calls=%async_computation.16 | async-start | bytes 4915200 | tf_op jit(solution)/shard_map/all_gather | solution.py:243
  575.0 229.0 %reduce-scatter.21.cloned.1.call-start = ((), (), s32[]{:S(2)}) async-start(), calls=%async_computation.17 | async-start | bytes 9830400 | tf_op jit(solution)/shard_map/reduce_scatter | solution.py:252
  652.1 11.6 copy-start.32
  669.2 219.9 %all-gather.18.cloned.1.call-start = ((), (), s32[]{:S(2)}) async-start(), calls=%async_computation.18 | async-start | bytes 4915200 | tf_op jit(solution)/shard_map/all_gather | solution.py:263
  809.7 79.4 %copy-start.16 = (bf16[768,192]{1,0:T(8,128)(2,1)S(1)}, bf16[768,192]{1,0:T(8,128)(2,1)}, u32[]{:S(2)}) copy-start(bf16[768,192]{1,0:T(8,128)(2,1)} %all_gather.71) | copy-start | bytes 884740
  812.0 393.1 %reduce-scatter.23.cloned.1.call-start = ((), (), s32[]{:S(2)}) async-start(), calls=%async_computation.19 | async-start | bytes 4915200 | tf_op jit(solution)/shard_map/reduce_scatter | solution.py:315
  969.8 10.5 copy-start.1
  1099.4 10.5 copy-start.1
  1126.2 117.9 %reduce-scatter.27.cloned.1.call-start = ((), (), s32[]{:S(2)}) async-start(), calls=%async_computation.21 | async-start | bytes 2654208 | tf_op jit(solution)/shard_map/reduce_scatter | solution.py:357
  1134.3 156.1 %reduce-scatter.29.cloned.1.call-start = ((), (), s32[]{:S(2)}) async-start(), calls=%async_computation.22 | async-start | bytes 2654208 | tf_op jit(solution)/shard_map/reduce_scatter | solution.py:358
  1142.4 186.7 %reduce-scatter.25.cloned.1.call-start = ((), (), s32[]{:S(2)}) async-start(), calls=%async_computation.20 | async-start | bytes 884736 | tf_op jit(solution)/shard_map/reduce_scatter | solution.py:356
  1146.8 221.0 %reduce-scatter.31.cloned.1.call-start = ((), (), s32[]{:S(2)}) async-start(), calls=%async_computation.23 | async-start | bytes 884736
  1151.8 254.6 %reduce-scatter.33.cloned.1.call-start = ((), (), s32[]{:S(2)}) async-start(), calls=%async_computation.24 | async-start | bytes 884736
  1156.0 289.1 %reduce-scatter.35.cloned.1.call-start = ((), (), s32[]{:S(2)}) async-start(), calls=%async_computation.25 | async-start | bytes 884736
  1161.7 43.4 %copy-start.13 = (f32[640,768]{1,0:T(8,128)S(1)}, f32[640,768]{1,0:T(8,128)}, u32[]{:S(2)}) copy-start(f32[640,768]{1,0:T(8,128)} %get-tuple-element.363) | copy-start | bytes 5898244
  (38 other events, 156.8 us)
Sparse Core Ops, SparseCore 0:
  10.4 79.1 all-gather.7
  184.3 134.8 reduce-scatter.16
  575.2 76.9 all-gather.15
  812.1 76.9 all-gather.17
  1126.3 71.1 reduce-scatter.22
  1201.3 42.7 reduce-scatter.26
  1248.0 42.3 reduce-scatter.28
  1294.1 34.9 reduce-scatter.24
  1332.8 34.9 reduce-scatter.30
  1371.4 34.9 reduce-scatter.32
  1410.1 34.9 reduce-scatter.34
Sparse Core Ops, SparseCore 1:
  186.6 22.3 all-gather.11
  323.1 76.8 all-gather.9
  401.7 22.3 all-gather.13
  433.0 136.2 reduce-scatter.18
  669.3 134.7 reduce-scatter.20
where the time goes:
time: 1460 us; the launch traced here: 1450 us
  waiting for transfers between devices  870 us (60%)
  matrix products  295 us (20%)
  other arithmetic  116 us (8%)
  blocking collectives  109 us (7%)
  local copies, waits for them, and re-layouts  42.9 us (3%)
  between operations  18.4 us (1%)
    reduce_scatter x1, waiting for transfers between devices, body(): lax.psum_scatter(contract_last(hidden, down_weight), 'tp', scatter_dimens...  136 us
    reduce_scatter x1, waiting for transfers between devices, body(): lax.psum_scatter(contract_last(grad_pre, up_weight), 'tp', scatter_dimens...  134 us
    reduce_scatter x1, waiting for transfers between devices, body(): lax.psum_scatter(contract_last(mixed_rows, out_weight), 'tp', scatter_dim...  134 us
    unnamed x19, waiting for transfers between devices  118 us
    all_gather x1, waiting for transfers between devices, body(): lax.all_gather(second_residual_gradient.astype(jnp.bfloat16), 'tp', axis=...  77 us
    all_gather x1, waiting for transfers between devices, body(): lax.all_gather(first_residual_gradient.astype(jnp.bfloat16), 'tp', axis=0...  76.9 us
    all_gather x1, waiting for transfers between devices, body(): lax.all_gather(normalized_rows.astype(jnp.bfloat16), 'tp', axis=0, tiled=...  67.2 us
    dot_general x10, matrix products, masked_scores(): jnp.einsum('qhd,khd->hqk', query_block, key_heads, preferred_element_type...  61.8 us
  transfers between devices with their start and end apart: 16, of which 14 were waited for; matrix products, arithmetic and copies ran while one was open for 6% of the time, Pallas kernels for 0%

commit v1 on v0

--- a/solution.py
+++ b/solution.py
@@ -1,3 +1,4 @@
+import functools
 import jax
 import jax.numpy as jnp
 from jax import lax
@@ -7,6 +8,37 @@
 EPS = 1e-05
 SQRT_HALF = 0.7071067811865476
 INV_ROOT_TAU = 0.3989422804014327
+
+
+def _link_ends(q_in, mesh_name, join_dim):
+    block_now = jax.lax.axis_size(mesh_name)
+    z1, arr_out, before = (block_now, jax.lax.axis_index(mesh_name), q_in.shape[join_dim])
+    entries = []
+    for dev_i in range(z1):
+        entries.append((dev_i, (dev_i + 1) % z1))
+    lanes = []
+    for dev_i in range(z1):
+        lanes.append((dev_i, (dev_i - 1) % z1))
+    carry_out = jnp.zeros(
+        (*q_in.shape[:join_dim], z1 * before, *q_in.shape[join_dim + 1 :]), q_in.dtype
+    )
+    carry_out = lax.dynamic_update_slice_in_dim(carry_out, q_in, arr_out * before, axis=join_dim)
+    front = row_out = q_in
+    frame_out = z1 // 2
+    for j in range(1, frame_out + 1):
+        front = jax.lax.ppermute(front, axis_name=mesh_name, perm=entries)
+        carry_out = lax.dynamic_update_slice_in_dim(
+            carry_out, front, (arr_out - j) % z1 * before, axis=join_dim
+        )
+        if j < z1 - frame_out:
+            row_out = jax.lax.ppermute(row_out, axis_name=mesh_name, perm=lanes)
+            carry_out = lax.dynamic_update_slice_in_dim(
+                carry_out, row_out, (arr_out + j) % z1 * before, axis=join_dim
+            )
+    return carry_out
+
+
+sites_shape = functools.partial(_link_ends, mesh_name="tp", join_dim=0)
 
 
 def normalize_layer(resid):
@@ -184,7 +216,7 @@
     normalized_rows = first_centered_scaled * first_norm_gain.astype(
         jnp.float32
     ) + first_norm_shift.astype(jnp.float32)
-    normed_full = lax.all_gather(normalized_rows.astype(jnp.bfloat16), "tp", axis=0, tiled=True)
+    normed_full = sites_shape(normalized_rows.astype(jnp.bfloat16))
     pre_act = jnp.dot(normed_full, up_weight, preferred_element_type=jnp.float32) + own_up_bias
     hidden = jax.nn.gelu(pre_act, approximate=False).astype(jnp.bfloat16)
     feedforward_term = lax.psum_scatter(

time: 1460 us -> 1450 us (level)
  waiting for transfers between devices: 870 us -> 832 us
  starting transfers between devices: 1.49 us -> 23.9 us
    all_gather x1 -> x0, waiting for transfers between devices: 67.2 us -> none  [body(): lax.all_gather(normalized_rows.astype(jnp.bfloat16), 'tp', axis=0, tiled=...]
    ppermute x0 -> x3, waiting for transfers between devices: none -> 31.7 us  [the longest x2 31.7 us: _link_ends(): front = jax.lax.ppermute(front, axis_name=mesh_name, perm=entries)]
    ppermute x0 -> x3, starting transfers between devices: none -> 22.4 us  [the longest x2 20 us: _link_ends(): front = jax.lax.ppermute(front, axis_name=mesh_name, perm=entries)]
    unnamed x19 -> x18, waiting for transfers between devices: 118 us -> 117 us
  transfers between devices with their start and end apart: 16 -> 18, of which waited for: 14 -> 14; matrix products, arithmetic and copies ran while one was open for 6% -> 6% of each run, Pallas kernels for 0% -> 0%
where the time goes in v1:
time: 1450 us
  waiting for transfers between devices  832 us (57%)
  matrix products  294 us (20%)
  other arithmetic  116 us (8%)
  blocking collectives  108 us (7%)
  local copies, waits for them, and re-layouts  52.6 us (4%)
  starting transfers between devices  23.9 us (2%)
  between operations  18.4 us (1%)
    reduce_scatter x1, waiting for transfers between devices, body(): lax.psum_scatter(contract_last(hidden, down_weight), 'tp', scatter_dimens...  135 us
    reduce_scatter x1, waiting for transfers between devices, body(): lax.psum_scatter(contract_last(grad_pre, up_weight), 'tp', scatter_dimens...  134 us
    reduce_scatter x1, waiting for transfers between devices, body(): lax.psum_scatter(contract_last(mixed_rows, out_weight), 'tp', scatter_dim...  134 us
    unnamed x18, waiting for transfers between devices  117 us
    all_gather x1, waiting for transfers between devices, body(): lax.all_gather(first_residual_gradient.astype(jnp.bfloat16), 'tp', axis=0...  77 us
    all_gather x1, waiting for transfers between devices, body(): lax.all_gather(second_residual_gradient.astype(jnp.bfloat16), 'tp', axis=...  76.9 us
    dot_general x10, matrix products, masked_scores(): jnp.einsum('qhd,khd->hqk', query_block, key_heads, preferred_element_type...  61.8 us
    unnamed x2, blocking collectives  53.1 us
  transfers between devices with their start and end apart: 18, of which 14 were waited for; matrix products, arithmetic and copies ran while one was open for 6% of the time, Pallas kernels for 0%

profile of v1, /device:TPU:0, one launch (start us, length us, event | category | flops | bytes accessed | tf_op | source)
XLA Modules:
  0.0 1445.5 jit_solution(10072454468113163312)
XLA Ops:
  18.3 27.4 %all-reduce.19 = (bf16[768]{0:T(1024)(128)(2,1)S(1)}, bf16[768]{0:T(1024)(128)(2,1)S(1)}, bf16[768]{0:T(1024)(128)(2,1)}, bf16[768]{0:T(1024)(128)(2,1)}, bf16[7...) all-reduce(bf16[768]{0:T(1024)(128)(2,1)S(1)} %dynamic-update-slice, ...), channel_id=1, replica_groups=mesh['dp'=8,'tp'=4] {'dp'}, use_global_device_ids=true, to_apply=%add | all-reduce | flops 6144 | bytes 24576
  72.6 10.4 all_gather.68
  103.3 72.3 %while.28 = (s32[]{:T(128)}, bf16[5,512,192]{1,2,0:T(8,128)(2,1)}, f32[5,3,512]{2,1,0:T(4,128)S(1)}, s32[5,512]{1,0:T(8,128)S(1)}, bf16[5,512,3,64]{1,3,2,0:T(8,...) while((s32[]{:T(128)}, bf16[5,512,192]{1,2,0:T(8,128)(2,1)}, ...), condition=%wide.region_4.5_spmd.clone, body=%wide.region_1.4_spmd.clone.sunk | while | flops 1055231488 | bytes 55263352 | solution.py:209
  185.3 133.8 %reduce-scatter.17.cloned.1.call-done = f32[640,768]{1,0:T(8,128)} async-done(((f32[2560,768]{1,0:T(8,128)}), f32[640,768]{1,0:T(8,128)}) %reduce-scatter.17.cloned.1.call-update) | async-done | bytes 1966096 | tf_op jit(solution)/shard_map/reduce_scatter | solution.py:211
  329.3 23.0 %collective-permute-done = bf16[640,768]{1,0:T(8,128)(2,1)} collective-permute-done((bf16[640,768]{1,0:T(8,128)(2,1)}, bf16[640,768]{1,0:T(8,128)(2,1)}, u32[]{:S(2)}, u32[]{:S(2)}) %collective-permute-start) | collective-permute-done | bytes 983072 | tf_op jit(solution)/shard_map/ppermute | solution.py:29
  352.3 18.6 %collective-permute-start.2 = (bf16[640,768]{1,0:T(8,128)(2,1)}, bf16[640,768]{1,0:T(8,128)(2,1)}, u32[]{:S(2)}, u32[]{:S(2)}) collective-permute-start(bf16[640,768]{1,0:T(8,128)(2,1)} %collective-permute-done), channel_id=1, source_target_pairs={{0,1},{1,2},{2,3},{3,0},{4,5},{5,6},{6,7},{7,4},{8,9},{9,10},{10,1... | collective-permute-start | bytes 2949128 | tf_op jit(solution)/shard_map/ppermute | solution.py:29
  395.5 22.3 %fusion.42 = (bf16[2560,768]{1,0:T(8,128)(2,1)}, f32[2560,768]{1,0:T(8,128)}) fusion(f32[768]{0:T(1024)S(1)} %dynamic-slice_convert_fusion, bf16[2560,768]{1,0:T(8,128)(2,1)} %constant_dynamic-update-slice_fusion, bf16[768,768]{1,0:T(8,128)(2,1)} %all-gather.9.cloned.1.call-done), kind=kOutput, calls=%fused_computation.56 | convolution fusion | flops 3149660160 | bytes 16911360 | tf_op jit(solution)/shard_map/dot_general | solution.py:220
  427.3 134.9 %reduce-scatter.19.cloned.1.call-done = f32[640,768]{1,0:T(8,128)} async-done(((f32[2560,768]{1,0:T(8,128)}), f32[640,768]{1,0:T(8,128)}) %reduce-scatter.19.cloned.1.call-update) | async-done | bytes 1966096 | tf_op jit(solution)/shard_map/reduce_scatter | solution.py:222
  568.2 76.9 %all-gather.13.cloned.1.call-done = bf16[2560,768]{1,0:T(8,128)(2,1)} async-done(((bf16[640,768]{1,0:T(8,128)(2,1)}), bf16[2560,768]{1,0:T(8,128)(2,1)}) %all-gather.13.cloned.1.call-update) | async-done | bytes 3932176 | tf_op jit(solution)/shard_map/all_gather | solution.py:275
  645.0 9.7 convert_reduce_fusion.1
  662.7 134.3 %reduce-scatter.21.cloned.1.call-done = f32[640,768]{1,0:T(8,128)} async-done(((f32[2560,768]{1,0:T(8,128)}), f32[640,768]{1,0:T(8,128)}) %reduce-scatter.21.cloned.1.call-update) | async-done | bytes 1966096 | tf_op jit(solution)/shard_map/reduce_scatter | solution.py:284
  804.9 77.0 %all-gather.15.cloned.1.call-done = bf16[2560,768]{1,0:T(8,128)(2,1)} async-done(((bf16[640,768]{1,0:T(8,128)(2,1)}), bf16[2560,768]{1,0:T(8,128)(2,1)}) %all-gather.15.cloned.1.call-update) | async-done | bytes 3932176 | tf_op jit(solution)/shard_map/all_gather | solution.py:295
  891.3 215.4 %while.29 = (s32[]{:T(128)}, f32[2560,3,64]{0,2,1:T(8,128)}, f32[2560,3,64]{0,2,1:T(8,128)}, bf16[5,512,192]{1,2,0:T(8,128)(2,1)}, bf16[5,512,3,64]{1,3,2,0:T(8,...) while((s32[]{:T(128)}, f32[2560,3,64]{0,2,1:T(8,128)}, ...), condition=%wide.region_18.19_spmd.clone, body=%wide.region_16.18_spmd.clone.sunk | while | flops 2555940352 | bytes 180019440 | solution.py:334
  910.6 9.5 multiply_convert_fusion.2
  953.1 9.5 multiply_convert_fusion.2
  996.3 9.5 multiply_convert_fusion.2
  1039.5 9.5 multiply_convert_fusion.2
  1161.4 25.8 %all-reduce.17 = (f32[768]{0:T(1024)S(1)}, f32[768]{0:T(1024)S(1)}, f32[768]{0:T(1024)S(1)}, f32[768]{0:T(1024)S(1)}, f32[768]{0:T(1024)S(1)}, /*index=5*/f32[30...) all-reduce(f32[768]{0:T(1024)S(1)} %dynamic_update_slice.36, ...), channel_id=9, replica_groups=mesh['dp'=8,'tp'=4] {'dp'}, use_global_device_ids=true, to_apply=%region_25.26.clone | all-reduce | flops 9216 | bytes 73728
  1200.6 36.5 %reduce-scatter.27.cloned.1.call-done = f32[96,768]{1,0:T(8,128)} async-done(((f32[768,768]{1,0:T(8,128)}), f32[96,768]{1,0:T(8,128)}) %reduce-scatter.27.cloned.1.call-update) | async-done | bytes 294928 | tf_op jit(solution)/shard_map/reduce_scatter | solution.py:389
  1237.1 46.3 %reduce-scatter.29.cloned.1.call-done = f32[96,768]{1,0:T(8,128)} async-done(((f32[768,768]{1,0:T(8,128)}), f32[96,768]{1,0:T(8,128)}) %reduce-scatter.29.cloned.1.call-update) | async-done | bytes 294928 | tf_op jit(solution)/shard_map/reduce_scatter | solution.py:390
  1283.4 38.6 %reduce-scatter.25.cloned.1.call-done = f32[96,192]{1,0:T(8,128)} async-done(((f32[768,192]{1,0:T(8,128)}), f32[96,192]{1,0:T(8,128)}) %reduce-scatter.25.cloned.1.call-update) | async-done | bytes 73744 | tf_op jit(solution)/shard_map/reduce_scatter | solution.py:388
  1322.0 38.7 %reduce-scatter.31.cloned.1.call-done = f32[96,192]{1,0:T(8,128)} async-done(((f32[768,192]{1,0:T(8,128)}), f32[96,192]{1,0:T(8,128)}) %reduce-scatter.31.cloned.1.call-update) | async-done | bytes 73744
  1360.7 38.5 %reduce-scatter.33.cloned.1.call-done = f32[96,192]{1,0:T(8,128)} async-done(((f32[768,192]{1,0:T(8,128)}), f32[96,192]{1,0:T(8,128)}) %reduce-scatter.33.cloned.1.call-update) | async-done | bytes 73744
  1399.2 38.7 %reduce-scatter.35.cloned.1.call-done = f32[96,192]{1,0:T(8,128)} async-done(((f32[768,192]{1,0:T(8,128)}), f32[96,192]{1,0:T(8,128)}) %reduce-scatter.35.cloned.1.call-update) | async-done | bytes 73744
  (330 shorter events, 457.4 us)
Async XLA Ops:
  8.0 81.6 %all-gather.7.cloned.1.call-start = ((), (), s32[]{:S(2)}) async-start(), calls=%async_computation.10 | async-start | bytes 4915200 | tf_op jit(solution)/shard_map/all_gather | solution.py:173
  8.8 310.3 %reduce-scatter.17.cloned.1.call-start = ((), (), s32[]{:S(2)}) async-start(), calls=%async_computation.11 | async-start | bytes 9830400 | tf_op jit(solution)/shard_map/reduce_scatter | solution.py:211
  54.5 38.7 %copy-start.19 = (bf16[768,192]{1,0:T(8,128)(2,1)}, bf16[768,192]{1,0:T(8,128)(2,1)S(1)}, u32[]{:S(2)}) copy-start(bf16[768,192]{1,0:T(8,128)(2,1)S(1)} %all_gather.63) | copy-start | bytes 884740
  63.7 33.4 %copy-start.14 = (bf16[768,192]{1,0:T(8,128)(2,1)}, bf16[768,192]{1,0:T(8,128)(2,1)S(1)}, u32[]{:S(2)}) copy-start(bf16[768,192]{1,0:T(8,128)(2,1)S(1)} %all_gather.65) | copy-start | bytes 884740
  72.6 28.3 %copy-start.17 = (bf16[768,192]{1,0:T(8,128)(2,1)}, bf16[768,192]{1,0:T(8,128)(2,1)S(1)}, u32[]{:S(2)}) copy-start(bf16[768,192]{1,0:T(8,128)(2,1)S(1)} %all_gather.66) | copy-start | bytes 884740
  184.1 211.4 %all-gather.9.cloned.1.call-start = ((), (), s32[]{:S(2)}) async-start(), calls=%async_computation.12 | async-start | bytes 1327104 | tf_op jit(solution)/shard_map/all_gather | solution.py:124
  184.7 233.1 %all-gather.11.cloned.1.call-start = ((), (), s32[]{:S(2)}) async-start(), calls=%async_computation.13 | async-start | bytes 1327104 | tf_op jit(solution)/shard_map/all_gather | solution.py:125
  321.6 49.4 %copy-start.31 = (bf16[384]{0:T(512)(128)(2,1)S(1)}, bf16[384]{0:T(512)(128)(2,1)}, u32[]{:S(2)}) copy-start(bf16[384]{0:T(512)(128)(2,1)} %param.34) | copy-start | bytes 2308
  325.5 26.8 %collective-permute-start = (bf16[640,768]{1,0:T(8,128)(2,1)}, bf16[640,768]{1,0:T(8,128)(2,1)}, u32[]{:S(2)}, u32[]{:S(2)}) collective-permute-start(bf16[640,768]{1,0:T(8,128)(2,1)} %get-tuple-element.368), channel_id=1, source_target_pairs={{0,1},{1,2},{2,3},{3,0},{4,5},{5,6},{6,7},{7,4},{8,9},{9,10},{10,1... | collective-permute-start | bytes 2949128 | tf_op jit(solution)/shard_map/ppermute | solution.py:29
  327.0 55.3 %collective-permute-start.1 = (bf16[640,768]{1,0:T(8,128)(2,1)}, bf16[640,768]{1,0:T(8,128)(2,1)}, u32[]{:S(2)}, u32[]{:S(2)}) collective-permute-start(bf16[640,768]{1,0:T(8,128)(2,1)} %get-tuple-element.368), channel_id=1, source_target_pairs={{0,3},{1,0},{2,1},{3,2},{4,7},{5,4},{6,5},{7,6},{8,11},{9,8},{10,9... | collective-permute-start | bytes 2949128 | tf_op jit(solution)/shard_map/ppermute | solution.py:34
  352.3 40.9 %collective-permute-start.2 = (bf16[640,768]{1,0:T(8,128)(2,1)}, bf16[640,768]{1,0:T(8,128)(2,1)}, u32[]{:S(2)}, u32[]{:S(2)}) collective-permute-start(bf16[640,768]{1,0:T(8,128)(2,1)} %collective-permute-done), channel_id=1, source_target_pairs={{0,1},{1,2},{2,3},{3,0},{4,5},{5,6},{6,7},{7,4},{8,9},{9,10},{10,1... | collective-permute-start | bytes 2949128 | tf_op jit(solution)/shard_map/ppermute | solution.py:29
  370.9 191.3 %reduce-scatter.19.cloned.1.call-start = ((), (), s32[]{:S(2)}) async-start(), calls=%async_computation.14 | async-start | bytes 9830400 | tf_op jit(solution)/shard_map/reduce_scatter | solution.py:222
  426.7 218.4 %all-gather.13.cloned.1.call-start = ((), (), s32[]{:S(2)}) async-start(), calls=%async_computation.15 | async-start | bytes 4915200 | tf_op jit(solution)/shard_map/all_gather | solution.py:275
  568.0 229.0 %reduce-scatter.21.cloned.1.call-start = ((), (), s32[]{:S(2)}) async-start(), calls=%async_computation.16 | async-start | bytes 9830400 | tf_op jit(solution)/shard_map/reduce_scatter | solution.py:284
  662.0 219.9 %all-gather.15.cloned.1.call-start = ((), (), s32[]{:S(2)}) async-start(), calls=%async_computation.17 | async-start | bytes 4915200 | tf_op jit(solution)/shard_map/all_gather | solution.py:295
  802.6 79.3 %copy-start.16 = (bf16[768,192]{1,0:T(8,128)(2,1)S(1)}, bf16[768,192]{1,0:T(8,128)(2,1)}, u32[]{:S(2)}) copy-start(bf16[768,192]{1,0:T(8,128)(2,1)} %all_gather.68) | copy-start | bytes 884740
  804.9 393.1 %reduce-scatter.23.cloned.1.call-start = ((), (), s32[]{:S(2)}) async-start(), calls=%async_computation.18 | async-start | bytes 4915200 | tf_op jit(solution)/shard_map/reduce_scatter | solution.py:347
  1119.1 118.1 %reduce-scatter.27.cloned.1.call-start = ((), (), s32[]{:S(2)}) async-start(), calls=%async_computation.20 | async-start | bytes 2654208 | tf_op jit(solution)/shard_map/reduce_scatter | solution.py:389
  1127.2 156.3 %reduce-scatter.29.cloned.1.call-start = ((), (), s32[]{:S(2)}) async-start(), calls=%async_computation.21 | async-start | bytes 2654208 | tf_op jit(solution)/shard_map/reduce_scatter | solution.py:390
  1135.3 186.7 %reduce-scatter.25.cloned.1.call-start = ((), (), s32[]{:S(2)}) async-start(), calls=%async_computation.19 | async-start | bytes 884736 | tf_op jit(solution)/shard_map/reduce_scatter | solution.py:388
  1139.6 221.1 %reduce-scatter.31.cloned.1.call-start = ((), (), s32[]{:S(2)}) async-start(), calls=%async_computation.22 | async-start | bytes 884736
  1144.6 254.6 %reduce-scatter.33.cloned.1.call-start = ((), (), s32[]{:S(2)}) async-start(), calls=%async_computation.23 | async-start | bytes 884736
  1148.9 289.0 %reduce-scatter.35.cloned.1.call-start = ((), (), s32[]{:S(2)}) async-start(), calls=%async_computation.24 | async-start | bytes 884736
  1154.6 43.3 %copy-start.13 = (f32[640,768]{1,0:T(8,128)S(1)}, f32[640,768]{1,0:T(8,128)}, u32[]{:S(2)}) copy-start(f32[640,768]{1,0:T(8,128)} %get-tuple-element.363) | copy-start | bytes 5898244
  (40 other events, 187.2 us)
Sparse Core Ops, SparseCore 0:
  10.4 79.1 all-gather.6
  184.2 134.8 reduce-scatter.16
  426.8 135.3 reduce-scatter.18
  568.1 76.9 all-gather.12
  662.2 134.7 reduce-scatter.20
  805.0 76.9 all-gather.14
  1119.2 71.1 reduce-scatter.22
  1194.3 42.7 reduce-scatter.26
  1241.1 42.3 reduce-scatter.28
  1287.0 34.9 reduce-scatter.24
  1325.7 34.9 reduce-scatter.30
  1364.3 34.9 reduce-scatter.32
  1403.0 34.9 reduce-scatter.34
Sparse Core Ops, SparseCore 1:
  186.5 22.3 all-gather.8
  371.0 24.4 all-gather.10
